TPU v7x, 32 devices: a whole 2x2x4 slice. The times are simulated.
32 devices in a mesh: tissue: 2 (over x), sample: 4 (over y, core), variant: 4 (over z).
Axes of the slice: x: 2, y: 2, z: 4, core: 2. Of those that a mesh axis runs over, the one named last changes fastest.
Arguments:
- dosage: bfloat16 [52, 512, 512], P('tissue', 'sample', 'variant'), may hold values from 0 to 2
- express: bfloat16 [52, 512, 2048], P('tissue', 'sample', 'variant'), may hold values from -6 to 6
- covar: float32 [52, 32, 512], P('tissue', None, 'sample'), may hold values from -6 to 6
- member: int32 [52, 512], P('tissue', 'sample'), may hold values 0 or 1
- live: int32 [52], replicated, may hold values 0 or 1
- mixing: float32 [52, 52], replicated, may hold values from -1 to 2, as said below
Outputs:
- chi_stat: float32 [512, 2048], P('variant', 'sample')
- meta_stat: float32 [512, 2048], P('variant', 'sample')
Inputs may be any that keep to these rules, and one draw needn't show every extreme that they name: mixing is the identity plus a dense spread of off-diagonal and diagonal terms.
All inputs are finite; a program needn't handle non-finite values. No bound on the sum of `member` on one device may be relied on, other than what follows from the above.
Results may differ from a plain program's by a relative error of at most 0.019.
Values may be sent and summed in bfloat16 or wider, within the bound.
A program may use at most 128 MiB of HBM per device.

v0:
```python
import jax
import jax.numpy as jnp
from jax import lax
from jax.sharding import PartitionSpec as P


def solve_small(factor_low, rhs_matrix):
    forward = lax.linalg.triangular_solve(factor_low, rhs_matrix, left_side=True, lower=True)
    return lax.linalg.triangular_solve(
        factor_low, forward, left_side=True, lower=True, transpose_a=True
    )


def body(dosage, express, covar, member, live, mixing):
    highest = lax.Precision.HIGHEST
    tis_dev = dosage.shape[0]
    n_cov = covar.shape[1]
    weights = member.astype(jnp.float32)
    dos_masked = dosage.astype(jnp.float32) * weights[:, :, None]
    cov_masked = covar * weights[:, None, :]
    gram_part = jnp.einsum("tks,tjs->tkj", cov_masked, cov_masked, precision=highest)
    amat_part = jnp.einsum("tks,tsv->tkv", cov_masked, dos_masked, precision=highest)
    count_part = jnp.sum(weights, axis=1)
    gsq_part = jnp.sum(dos_masked * dos_masked, axis=1)
    identity = jnp.eye(n_cov, dtype=jnp.float32)
    gathered = lax.all_gather(express, "variant", axis=2, tiled=True)
    exp_masked = gathered.astype(jnp.float32) * weights[:, :, None]
    bmat_part = jnp.einsum("tks,tsg->tkg", cov_masked, exp_masked, precision=highest)
    esq_part = jnp.sum(exp_masked * exp_masked, axis=1)
    gram_sum, amat_sum, counts, gsq_sum, bmat_sum, esq_sum = (
        lax.psum(gram_part.astype(jnp.bfloat16), "sample").astype(jnp.float32),
        lax.psum(amat_part.astype(jnp.bfloat16), "sample").astype(jnp.float32),
        lax.psum(count_part.astype(jnp.bfloat16), "sample").astype(jnp.float32),
        lax.psum(gsq_part.astype(jnp.bfloat16), "sample").astype(jnp.float32),
        lax.psum(bmat_part.astype(jnp.bfloat16), "sample").astype(jnp.float32),
        lax.psum(esq_part.astype(jnp.bfloat16), "sample").astype(jnp.float32),
    )
    factor_low = jnp.linalg.cholesky(gram_sum + identity)
    proj_exp = solve_small(factor_low, bmat_sum)
    eres = (
        exp_masked - jnp.einsum("tks,tkg->tsg", cov_masked, proj_exp, precision=highest)
    ).astype(jnp.bfloat16)
    enorm = esq_sum - jnp.sum(bmat_sum * proj_exp, axis=1)
    proj_dos = solve_small(factor_low, amat_sum)
    gres = (
        dos_masked - jnp.einsum("tks,tkv->tsv", cov_masked, proj_dos, precision=highest)
    ).astype(jnp.bfloat16)
    gnorm = gsq_sum - jnp.sum(amat_sum * proj_dos, axis=1)
    n_genes = eres.shape[2]
    gene_share = n_genes // lax.axis_size("sample")
    cross = lax.psum_scatter(
        jnp.einsum("tse,tsv->etv", eres, gres, preferred_element_type=jnp.float32).astype(
            jnp.bfloat16
        ),
        "sample",
        scatter_dimension=0,
        tiled=True,
    ).astype(jnp.float32)
    gene_start = lax.axis_index("sample") * gene_share
    enorm_slice = lax.dynamic_slice_in_dim(enorm, gene_start, gene_share, 1)
    tissue_start = lax.axis_index("tissue") * tis_dev
    live_f = live.astype(jnp.float32)
    live_own = lax.dynamic_slice_in_dim(live_f, tissue_start, tis_dev, 0)
    scales = live_own * jnp.sqrt(jnp.maximum(counts - n_cov, 1.0))
    inv_var = 1.0 / jnp.sqrt(gnorm + 1e-05)
    inv_gene = 1.0 / jnp.sqrt(enorm_slice + 1e-05)
    zvals = (
        cross * scales[None, :, None] * inv_var[None, :, :] * jnp.transpose(inv_gene)[:, :, None]
    )
    own_rows = lax.dynamic_slice_in_dim(mixing, tissue_start, tis_dev, 0)
    mixed = jnp.zeros_like(zvals) + jnp.einsum(
        "ut,gtv->guv",
        own_rows,
        lax.all_gather(zvals.astype(jnp.bfloat16), "tissue", axis=1, tiled=True).astype(
            jnp.float32
        ),
        precision=highest,
    )
    mixed = mixed * live_own[None, :, None]
    nlive = jnp.maximum(jnp.sum(live_f), 1.0)
    chi_part = jnp.sum(mixed * mixed, axis=1) / nlive
    meta_part = jnp.sum(mixed, axis=1) / jnp.sqrt(nlive)
    chi_stat, meta_stat = (
        lax.psum(chi_part.astype(jnp.bfloat16), "tissue").astype(jnp.float32),
        lax.psum(meta_part.astype(jnp.bfloat16), "tissue").astype(jnp.float32),
    )
    return (jnp.transpose(chi_stat), jnp.transpose(meta_stat))


def solution(mesh):
    return jax.shard_map(
        body,
        mesh=mesh,
        in_specs=(
            P("tissue", "sample", "variant"),
            P("tissue", "sample", "variant"),
            P("tissue", None, "sample"),
            P("tissue", "sample"),
            P(),
            P(),
        ),
        out_specs=(P("variant", "sample"), P("variant", "sample")),
        check_vma=False,
    )
```

profile of v0, /device:TPU:0, one launch (start us, length us, event | category | flops | bytes accessed | tf_op | source)
XLA Modules:
  0.0 751.9 jit_solution(18436027038904383437)
XLA Ops:
  8.7 3.7 fusion.8
  12.4 235.3 %all-gather.3.cloned.1.call-done = bf16[26,128,2048]{2,1,0:T(8,128)(2,1)} async-done(((bf16[26,128,512]{2,1,0:T(8,128)(2,1)}), bf16[26,128,2048]{2,1,0:T(8,128)(2,1)}) %all-gather.3.cloned.1.call-update) | async-done | bytes 13631504 | tf_op jit(solution)/shard_map/all_gather | solution.py:26
  247.6 19.7 %fusion.6 = bf16[26,32,2048]{2,1,0:T(8,128)(2,1)} fusion(bf16[26,128,2048]{2,1,0:T(8,128)(2,1)} %all-gather.3.cloned.1.call-done, f32[26,128]{1,0:T(8,128)S(1)} %convert_element_type.83, f32[26,32,128]{2,1,0:T(8,128)} %param.8), kind=kOutput, calls=%fused_computation.14 | convolution fusion | flops 2632687616 | bytes 17478656 | tf_op jit(solution)/shard_map/tks,tsg->tkg/dot_general | solution.py:28
  267.4 10.8 %multiply_reduce_fusion = bf16[26,2048]{1,0:T(8,128)(2,1)} fusion(bf16[26,128,2048]{2,1,0:T(8,128)(2,1)} %all-gather.3.cloned.1.call-done, f32[26,128]{1,0:T(8,128)S(1)} %convert_element_type.83), kind=kLoop, calls=%fused_computation | loop fusion | flops 27209728 | bytes 13751296 | tf_op jit(solution)/shard_map/reduce_sum | solution.py:29
  278.2 10.6 %reduce-scatter.2.cloned.1.call-start = ((), (), s32[]{:S(2)}) async-start(), calls=%async_computation.2 | async-start | bytes 17039360 | tf_op jit(solution)/shard_map/reduce_scatter | solution.py:51
  289.5 0.8 convolution_convert_fusion.1
  290.3 19.6 %all-reduce = (bf16[26,32,32]{1,2,0:T(8,128)(2,1)S(1)}, bf16[26,128]{1,0:T(8,128)(2,1)S(1)}, bf16[26]{0:T(256)(128)(2,1)S(1)}) all-reduce(bf16[26,32,32]{1,2,0:T(8,128)(2,1)S(1)} %convolution_convert_fusion.1, bf16[26,128]{1,0:T(8,128)(2,1)S(1)} %multiply_reduce_fusion.2, ...), channel_id=1, replica_groups=mesh['tissue'=2,'sample'=4,'variant'=4] {'sample'}, use_global_device_ids=true, to_apply=%region_0.0 | all-reduce | flops 29978 | bytes 119912 | tf_op jit(solution)/shard_map/psum | solution.py:31
  310.2 76.2 %custom-call.13 = f32[26,32,32]{2,1,0:T(8,128)S(1)} custom-call(f32[26,32,32]{2,1,0:T(8,128)S(1)} %fusion.18), custom_call_target="Cholesky" | custom-call | tf_op jit(solution)/shard_map/jit(cholesky)/cholesky | solution.py:38
  386.7 64.7 %custom-call.14 = f32[26,1,32,32]{2,3,1,0:T(8,128)} custom-call(f32[26,1,32,32]{3,2,1,0:T(8,128)S(1)} %select_bitcast_fusion), custom_call_target="InvertDiagBlocksLowerTriangular" | custom-call | tf_op jit(solution)/shard_map/triangular_solve | solution.py:9
  451.5 5.2 fusion.12
  456.8 8.4 %multiply_reduce_fusion.1 = (f32[26,2048]{1,0:T(8,128)}, f32[26,32,2048]{2,1,0:T(8,128)S(1)}) fusion(bf16[26,32,2048]{2,1,0:T(8,128)(2,1)S(1)} %copy-done.3, f32[26,32,2048]{2,1,0:T(8,128)S(1)} %fusion.12, f32[26,1,32,32]{2,3,1,0:T(8,128)S(1)} %copy-done.6), kind=kOutput, calls=%fused_computation.13 | convolution fusion | flops 659369984 | bytes 17358848 | tf_op jit(solution)/shard_map/triangular_solve | solution.py:9
  466.3 3.4 subtract_convert_fusion.1
  469.7 27.1 %subtract_convert_fusion = bf16[26,128,2048]{2,1,0:T(8,128)(2,1)} fusion(bf16[26,128,2048]{2,1,0:T(8,128)(2,1)S(1)} %bitcast.46, f32[26,32,2048]{2,1,0:T(8,128)S(1)} %get-tuple-element.19, f32[26,128]{1,0:T(8,128)S(1)} %convert_element_type.83, f32[26,32,128]{2,1,0:T(8,128)} %param.8), kind=kOutput, calls=%fused_computation.1 | convolution fusion | flops 2644615168 | bytes 34518016 | tf_op jit(solution)/shard_map/tks,tkg->tsg/dot_general | solution.py:41
  496.8 13.5 %fusion.2 = bf16[2048,26,128]{0,2,1:T(8,128)(2,1)} fusion(bf16[26,128,128]{2,1,0:T(8,128)(2,1)S(1)} %subtract_convert_fusion.1, bf16[26,128,2048]{2,1,0:T(8,128)(2,1)} %subtract_convert_fusion), kind=kOutput, calls=%fused_computation.6 | convolution fusion | flops 1751646208 | bytes 28114944 | tf_op jit(solution)/shard_map/tse,tsv->etv/dot_general | solution.py:52
  511.1 0.9 fusion.33
  511.9 99.5 %reduce-scatter.2.cloned.1.call-done = bf16[512,26,128]{0,2,1:T(8,128)(2,1)} async-done(((bf16[2048,26,128]{0,2,1:T(8,128)(2,1)}), bf16[512,26,128]{0,2,1:T(8,128)(2,1)}) %reduce-scatter.2.cloned.1.call-update) | async-done | bytes 3407888 | tf_op jit(solution)/shard_map/reduce_scatter | solution.py:51
  611.4 2.8 multiply_convert_fusion
  614.2 3.6 copy.23
  619.2 85.1 %all-gather.5.cloned.1.call-done = bf16[512,52,128]{2,0,1:T(8,128)(2,1)} async-done(((bf16[512,26,128]{2,0,1:T(8,128)(2,1)}), bf16[512,52,128]{2,0,1:T(8,128)(2,1)}) %all-gather.5.cloned.1.call-update) | async-done | bytes 6815760 | tf_op jit(solution)/shard_map/all_gather | solution.py:74
  704.3 12.9 %bitcast_reduce_fusion = (f32[512,128]{1,0:T(8,128)S(1)}, f32[512,128]{1,0:T(8,128)S(1)}) fusion(f32[26]{0:T(128)S(1)} %get-tuple-element.17, f32[52,52]{1,0:T(8,128)S(1)} %copy-done, s32[]{:T(128)S(6)} %select_n.12, bf16[512,52,128]{2,0,1:T(8,128)(2,1)} %all-gather.5.cloned.1.call-done), kind=kOutput, calls=%fused_computation.7 | convolution fusion | flops 1069940736 | bytes 7356932 | tf_op jit(solution)/shard_map/ut,gtv->guv/dot_general | solution.py:71
  717.2 0.8 fusion.29
  718.0 23.5 %all-reduce.8.cloned.1.call-done = (bf16[128,512]{0,1:T(8,128)(2,1)}, bf16[128,512]{0,1:T(8,128)(2,1)}) async-done(((bf16[128,512]{0,1:T(8,128)(2,1)}, bf16[128,512]{0,1:T(8,128)(2,1)}), (bf16[128,512]{0,1:T(8,128)(2,1)}, bf16[128,512]{0,1:T(8,128)(2,1)})) %all-reduce.8.cloned.1.call-update) | async-done | bytes 262160 | tf_op jit(solution)/shard_map/psum | solution.py:84
  741.5 1.7 copy.25
  743.2 1.7 copy.26
  (58 shorter events, 5.4 us)
Async XLA Ops:
  7.2 697.1 %copy-start = (f32[52,52]{1,0:T(8,128)S(1)}, f32[52,52]{1,0:T(8,128)}, u32[]{:S(2)}) copy-start(f32[52,52]{1,0:T(8,128)} %param.11) | copy-start | bytes 32452
  7.2 240.5 %all-gather.3.cloned.1.call-start = ((), (), s32[]{:S(2)}) async-start(), calls=%async_computation.1 | async-start | bytes 17039360 | tf_op jit(solution)/shard_map/all_gather | solution.py:26
  7.9 443.5 %all-reduce.6.cloned.1.call-start = ((), (), s32[]{:S(2)}) async-start(), calls=%async_computation.4 | async-start | bytes 7503872 | tf_op jit(solution)/shard_map/psum | solution.py:32
  267.4 21.5 %copy-start.8 = (s32[26,128]{1,0:T(8,128)S(1)}, s32[26,128]{1,0:T(8,128)}, u32[]{:S(2)}) copy-start(s32[26,128]{1,0:T(8,128)} %param.9) | copy-start | bytes 39940
  267.4 21.6 %copy-start.4 = (bf16[26,128,128]{2,1,0:T(8,128)(2,1)S(1)}, bf16[26,128,128]{2,1,0:T(8,128)(2,1)}, u32[]{:S(2)}) copy-start(bf16[26,128,128]{2,1,0:T(8,128)(2,1)} %param.6) | copy-start | bytes 2555908
  267.4 22.1 %copy-start.1 = (f32[26,32,128]{2,1,0:T(8,128)S(1)}, f32[26,32,128]{2,1,0:T(8,128)}, u32[]{:S(2)}) copy-start(f32[26,32,128]{2,1,0:T(8,128)} %param.8) | copy-start | bytes 1277956
  278.2 333.2 %reduce-scatter.2.cloned.1.call-start = ((), (), s32[]{:S(2)}) async-start(), calls=%async_computation.2 | async-start | bytes 17039360 | tf_op jit(solution)/shard_map/reduce_scatter | solution.py:51
  451.4 5.2 copy-start.3
  451.4 5.3 copy-start.6
  451.5 18.2 %slice-start = ((s8[13631488]{0:T(1024)(128)(4,1)}), s8[4194304]{0:T(1024)(128)(4,1)S(1)}, s32[]{:S(2)}) async-start(s8[13631488]{0:T(1024)(128)(4,1)} %bitcast.45), calls=%async_computation.6 | async-start | bytes 8388608
  451.5 18.2 %slice-start.1 = ((s8[13631488]{0:T(1024)(128)(4,1)}), s8[4194304]{0:T(1024)(128)(4,1)S(1)}, s32[]{:S(2)}) async-start(s8[13631488]{0:T(1024)(128)(4,1)} %bitcast.45), calls=%async_computation.7 | async-start | bytes 8388608
  456.7 8.4 %copy-start.7 = (bf16[26,32,128]{2,1,0:T(8,128)(2,1)S(1)}, bf16[26,32,128]{2,1,0:T(8,128)(2,1)}, u32[]{:S(2)}) copy-start(bf16[26,32,128]{2,1,0:T(8,128)(2,1)} %get-tuple-element.11) | copy-start | bytes 638980
  456.7 9.5 %copy-start.2 = (f32[26,32,128]{2,1,0:T(8,128)S(1)}, f32[26,32,128]{2,1,0:T(8,128)}, u32[]{:S(2)}) copy-start(f32[26,32,128]{2,1,0:T(8,128)} %param.8) | copy-start | bytes 1277956
  456.7 9.5 %copy-start.5 = (bf16[26,128,128]{2,1,0:T(8,128)(2,1)S(1)}, bf16[26,128,128]{2,1,0:T(8,128)(2,1)}, u32[]{:S(2)}) copy-start(bf16[26,128,128]{2,1,0:T(8,128)(2,1)} %param.6) | copy-start | bytes 2555908
  456.7 13.0 %slice-start.2 = ((s8[13631488]{0:T(1024)(128)(4,1)}), s8[4194304]{0:T(1024)(128)(4,1)S(1)}, s32[]{:S(2)}) async-start(s8[13631488]{0:T(1024)(128)(4,1)} %bitcast.45), calls=%async_computation.8 | async-start | bytes 8388608
  456.8 13.0 %slice-start.3 = ((s8[13631488]{0:T(1024)(128)(4,1)}), s8[1048576]{0:T(1024)(128)(4,1)S(1)}, s32[]{:S(2)}) async-start(s8[13631488]{0:T(1024)(128)(4,1)} %bitcast.45), calls=%async_computation.9 | async-start | bytes 2097152
  510.3 0.7 copy-start.9
  510.4 193.9 %all-gather.5.cloned.1.call-start = ((), (), s32[]{:S(2)}) async-start(), calls=%async_computation.3 | async-start | bytes 10223616 | tf_op jit(solution)/shard_map/all_gather | solution.py:74
  617.9 123.6 %all-reduce.8.cloned.1.call-start = ((), (), s32[]{:S(2)}) async-start(), calls=%async_computation.5 | async-start | bytes 524288 | tf_op jit(solution)/shard_map/psum | solution.py:84
Sparse Core Ops, SparseCore 0:
  9.6 238.0 all-gather.2
  278.3 80.5 all-reduce.5
  510.5 100.8 reduce-scatter.1
  618.0 86.2 all-gather.4
  718.1 23.3 all-reduce.7
where the time goes:
time: 760 us; the launch traced here: 752 us
  waiting for transfers between devices  444 us (58%)
  other arithmetic  159 us (21%)
  matrix products  95.8 us (13%)
  blocking collectives  19.6 us (3%)
  between operations  15.2 us (2%)
  starting transfers between devices  10.7 us (1%)
  local copies, waits for them, and re-layouts  7.88 us (1%)
    all_gather x1, waiting for transfers between devices, body(): gathered = lax.all_gather(express, 'variant', axis=2, tiled=True)  235 us
    reduce_scatter x1, waiting for transfers between devices, body(): lax.psum_scatter(jnp.einsum('tse,tsv->etv', eres, gres, preferred_element...  99.5 us
    all_gather x1, waiting for transfers between devices, body(): lax.all_gather(zvals.astype(jnp.bfloat16), 'tissue', axis=1, tiled=True)  85.1 us
    another operation x4, other arithmetic, body(): factor_low = jnp.linalg.cholesky(gram_sum + identity)  76.4 us
    another operation x3, other arithmetic, solve_small(): lax.linalg.triangular_solve(factor_low, forward, left_side=True, lower=Tr...  64.9 us
    dot_general x1, matrix products, body(): jnp.einsum('tks,tkg->tsg', cov_masked, proj_exp, precision=highest)  27.1 us
    psum x1, waiting for transfers between devices, body(): lax.psum(chi_part.astype(jnp.bfloat16), 'tissue').astype(jnp.float32)  23.5 us
    dot_general x1, matrix products, body(): jnp.einsum('tks,tsg->tkg', cov_masked, exp_masked, precision=highest)  19.7 us
  transfers between devices with their start and end apart: 5, of which 4 were waited for; matrix products, arithmetic and copies ran while one was open for 20% of the time, Pallas kernels for 0%

commit v1 on v0

--- a/solution.py
+++ b/solution.py
@@ -23,7 +23,16 @@
     count_part = jnp.sum(weights, axis=1)
     gsq_part = jnp.sum(dos_masked * dos_masked, axis=1)
     identity = jnp.eye(n_cov, dtype=jnp.float32)
-    gathered = lax.all_gather(express, "variant", axis=2, tiled=True)
+    dev_n = lax.axis_size("variant")
+    pages = [express]
+    for to_i in range(1, dev_n):
+        t1 = lax.ppermute(
+            pages[to_i - 1], "variant", [(nth, (nth - 1) % dev_n) for nth in range(dev_n)]
+        )
+        pages.append(t1)
+    u1 = jnp.concatenate(pages, 2)
+    v_next = lax.axis_index("variant")
+    gathered = jnp.roll(u1, v_next * express.shape[2], 2)
     exp_masked = gathered.astype(jnp.float32) * weights[:, :, None]
     bmat_part = jnp.einsum("tks,tsg->tkg", cov_masked, exp_masked, precision=highest)
     esq_part = jnp.sum(exp_masked * exp_masked, axis=1)

time: 760 us -> 763 us (level)
  local copies, waits for them, and re-layouts: 7.88 us -> 30.4 us
  waiting for transfers between devices: 444 us -> 422 us
    all_gather x1 -> x0, waiting for transfers between devices: 235 us -> none  [body(): gathered = lax.all_gather(express, 'variant', axis=2, tiled=True)]
    ppermute x0 -> x3, waiting for transfers between devices: none -> 208 us  [body(): lax.ppermute(pages[to_i - 1], 'variant', [(nth, (nth - 1) % dev_n) for nt...]
    unnamed x30 -> x31, local copies, waits for them, and re-layouts: 4.06 us -> 24.2 us
    ppermute x0 -> x3, starting transfers between devices: none -> 13.7 us  [body(): lax.ppermute(pages[to_i - 1], 'variant', [(nth, (nth - 1) % dev_n) for nt...]
    reduce_scatter x1, starting transfers between devices: 10.6 us -> 0.04 us  [body(): lax.psum_scatter(jnp.einsum('tse,tsv->etv', eres, gres, preferred_element...]
  transfers between devices with their start and end apart: 5 -> 7, of which waited for: 4 -> 6; matrix products, arithmetic and copies ran while one was open for 20% -> 20% of each run, Pallas kernels for 0% -> 0%
where the time goes in v1:
time: 763 us; the launch traced here: 759 us
  waiting for transfers between devices  422 us (55%)
  other arithmetic  159 us (21%)
  matrix products  103 us (13%)
  local copies, waits for them, and re-layouts  30.4 us (4%)
  blocking collectives  15.8 us (2%)
  between operations  15 us (2%)
  starting transfers between devices  13.9 us (2%)
    ppermute x3, waiting for transfers between devices, body(): lax.ppermute(pages[to_i - 1], 'variant', [(nth, (nth - 1) % dev_n) for nt...  208 us
    reduce_scatter x1, waiting for transfers between devices, body(): lax.psum_scatter(jnp.einsum('tse,tsv->etv', eres, gres, preferred_element...  105 us
    all_gather x1, waiting for transfers between devices, body(): lax.all_gather(zvals.astype(jnp.bfloat16), 'tissue', axis=1, tiled=True)  85.1 us
    another operation x4, other arithmetic, body(): factor_low = jnp.linalg.cholesky(gram_sum + identity)  76.4 us
    another operation x3, other arithmetic, solve_small(): lax.linalg.triangular_solve(factor_low, forward, left_side=True, lower=Tr...  64.8 us
    dot_general x1, matrix products, body(): jnp.einsum('tks,tkg->tsg', cov_masked, proj_exp, precision=highest)  28.2 us
    unnamed x31, local copies, waits for them, and re-layouts  24.2 us
    psum x1, waiting for transfers between devices, body(): lax.psum(chi_part.astype(jnp.bfloat16), 'tissue').astype(jnp.float32)  23.5 us
  transfers between devices with their start and end apart: 7, of which 6 were waited for; matrix products, arithmetic and copies ran while one was open for 20% of the time, Pallas kernels for 0%

profile of v1, /device:TPU:0, one launch (start us, length us, event | category | flops | bytes accessed | tf_op | source)
XLA Modules:
  0.0 759.2 jit_solution(11523505248698018070)
XLA Ops:
  7.2 5.1 collective-permute-start
  12.4 73.3 %collective-permute-done = bf16[26,128,512]{2,1,0:T(8,128)(2,1)S(1)} collective-permute-done((bf16[26,128,512]{2,1,0:T(8,128)(2,1)}, bf16[26,128,512]{2,1,0:T(8,128)(2,1)S(1)}, u32[]{:S(2)}, u32[]{:S(2)}) %collective-permute-start) | collective-permute-done | bytes 3407904 | tf_op jit(solution)/shard_map/ppermute | solution.py:29
  85.6 4.2 collective-permute-start.1
  89.8 72.1 %collective-permute-done.1 = bf16[26,128,512]{2,1,0:T(8,128)(2,1)} collective-permute-done((bf16[26,128,512]{2,1,0:T(8,128)(2,1)S(1)}, bf16[26,128,512]{2,1,0:T(8,128)(2,1)}, u32[]{:S(2)}, u32[]{:S(2)}) %collective-permute-start.1) | collective-permute-done | bytes 3407904 | tf_op jit(solution)/shard_map/ppermute | solution.py:29
  161.9 4.4 collective-permute-start.2
  172.4 2.5 constant_dynamic-update-slice_fusion.5
  175.0 62.9 %collective-permute-done.2 = bf16[26,128,512]{2,1,0:T(8,128)(2,1)} collective-permute-done((bf16[26,128,512]{2,1,0:T(8,128)(2,1)}, bf16[26,128,512]{2,1,0:T(8,128)(2,1)}, u32[]{:S(2)}, u32[]{:S(2)}) %collective-permute-start.2) | collective-permute-done | bytes 3407904 | tf_op jit(solution)/shard_map/ppermute | solution.py:29
  246.1 9.0 %copy-done.1 = bf16[26,128,4096]{2,1,0:T(8,128)(2,1)} copy-done((bf16[26,128,4096]{2,1,0:T(8,128)(2,1)}, bf16[26,128,4096]{2,1,0:T(8,128)(2,1)S(1)}, u32[]{:S(2)}) %copy-start.1) | copy-done | bytes 27263000
  255.1 18.0 %fusion.7 = bf16[26,32,2048]{2,1,0:T(8,128)(2,1)} fusion(f32[26,128]{1,0:T(8,128)S(1)} %convert_element_type.83, bf16[26,128,4096]{2,1,0:T(8,128)(2,1)S(1)} %constant_dynamic-update-slice_fusion, s32[]{:T(128)S(6)} %select_n.26, f32[26,32,128]{2,1,0:T(8,128)S(1)} %copy-done.4), kind=kOutput, calls=%fused_computation.15 | convolution fusion | flops 2632687616 | bytes 17498116 | tf_op jit(solution)/shard_map/tks,tsg->tkg/dot_general | solution.py:37
  273.1 10.8 %multiply_reduce_fusion = bf16[26,2048]{1,0:T(8,128)(2,1)} fusion(f32[26,128]{1,0:T(8,128)S(1)} %convert_element_type.83, bf16[26,128,4096]{2,1,0:T(8,128)(2,1)} %copy-done.1, s32[]{:T(128)S(6)} %select_n.26), kind=kLoop, calls=%fused_computation | loop fusion | flops 27209728 | bytes 13751300 | tf_op jit(solution)/shard_map/reduce_sum | solution.py:38
  285.5 15.8 %all-reduce = (bf16[26,32,32]{1,2,0:T(8,128)(2,1)S(1)}, bf16[26,128]{1,0:T(8,128)(2,1)S(1)}, bf16[26]{0:T(256)(128)(2,1)S(1)}) all-reduce(bf16[26,32,32]{1,2,0:T(8,128)(2,1)S(1)} %convolution_convert_fusion.1, bf16[26,128]{1,0:T(8,128)(2,1)S(1)} %multiply_reduce_fusion.2, ...), channel_id=1, replica_groups=mesh['tissue'=2,'sample'=4,'variant'=4] {'sample'}, use_global_device_ids=true, to_apply=%region_0.0 | all-reduce | flops 29978 | bytes 119912 | tf_op jit(solution)/shard_map/psum | solution.py:40
  301.7 76.2 %custom-call.13 = f32[26,32,32]{2,1,0:T(8,128)S(1)} custom-call(f32[26,32,32]{2,1,0:T(8,128)S(1)} %fusion.19), custom_call_target="Cholesky" | custom-call | tf_op jit(solution)/shard_map/jit(cholesky)/cholesky | solution.py:47
  378.2 64.7 %custom-call.14 = f32[26,1,32,32]{2,3,1,0:T(8,128)} custom-call(f32[26,1,32,32]{3,2,1,0:T(8,128)S(1)} %select_bitcast_fusion), custom_call_target="InvertDiagBlocksLowerTriangular" | custom-call | tf_op jit(solution)/shard_map/triangular_solve | solution.py:9
  442.9 6.7 fusion.13
  449.6 12.6 %multiply_reduce_fusion.1 = (f32[26,2048]{1,0:T(8,128)}, f32[26,32,2048]{2,1,0:T(8,128)}) fusion(bf16[26,32,2048]{2,1,0:T(8,128)(2,1)} %get-tuple-element.12, f32[26,32,2048]{2,1,0:T(8,128)} %fusion.13, f32[26,1,32,32]{2,3,1,0:T(8,128)S(1)} %copy-done.8), kind=kOutput, calls=%fused_computation.14 | convolution fusion | flops 659369984 | bytes 17358848 | tf_op jit(solution)/shard_map/triangular_solve | solution.py:9
  462.2 28.2 %subtract_convert_fusion = bf16[26,128,2048]{2,1,0:T(8,128)(2,1)} fusion(f32[26,32,2048]{2,1,0:T(8,128)} %get-tuple-element.19, f32[26,128]{1,0:T(8,128)S(1)} %convert_element_type.83, bf16[26,128,4096]{2,1,0:T(8,128)(2,1)S(1)} %copy-done.2, s32[]{:T(128)S(6)} %select_n.26, f32[26,32,128]{2,1,0:T(8,128)} %param.8), kind=kOutput, calls=%fused_computation.1 | convolution fusion | flops 2644615168 | bytes 34537476 | tf_op jit(solution)/shard_map/tks,tkg->tsg/dot_general | solution.py:50
  493.7 4.5 subtract_convert_fusion.1
  498.1 13.5 %fusion.2 = bf16[2048,26,128]{0,2,1:T(8,128)(2,1)} fusion(bf16[26,128,128]{2,1,0:T(8,128)(2,1)S(1)} %subtract_convert_fusion.1, bf16[26,128,2048]{2,1,0:T(8,128)(2,1)} %subtract_convert_fusion), kind=kOutput, calls=%fused_computation.6 | convolution fusion | flops 1751646208 | bytes 28114944 | tf_op jit(solution)/shard_map/tse,tsv->etv/dot_general | solution.py:61
  513.3 105.4 %reduce-scatter.2.cloned.1.call-done = bf16[512,26,128]{0,2,1:T(8,128)(2,1)} async-done(((bf16[2048,26,128]{0,2,1:T(8,128)(2,1)}), bf16[512,26,128]{0,2,1:T(8,128)(2,1)}) %reduce-scatter.2.cloned.1.call-update) | async-done | bytes 3407888 | tf_op jit(solution)/shard_map/reduce_scatter | solution.py:60
  618.6 2.8 multiply_convert_fusion
  621.5 3.6 copy.23
  626.4 85.1 %all-gather.2.cloned.1.call-done = bf16[512,52,128]{2,0,1:T(8,128)(2,1)} async-done(((bf16[512,26,128]{2,0,1:T(8,128)(2,1)}), bf16[512,52,128]{2,0,1:T(8,128)(2,1)}) %all-gather.2.cloned.1.call-update) | async-done | bytes 6815760 | tf_op jit(solution)/shard_map/all_gather | solution.py:83
  711.5 13.1 %bitcast_reduce_fusion = (f32[512,128]{1,0:T(8,128)S(1)}, f32[512,128]{1,0:T(8,128)S(1)}) fusion(f32[26]{0:T(128)S(1)} %get-tuple-element.17, f32[52,52]{1,0:T(8,128)S(1)} %copy-done, s32[]{:T(128)S(6)} %select_n.27, bf16[512,52,128]{2,0,1:T(8,128)(2,1)} %all-gather.2.cloned.1.call-done), kind=kOutput, calls=%fused_computation.8 | convolution fusion | flops 1069940736 | bytes 7356932 | tf_op jit(solution)/shard_map/ut,gtv->guv/dot_general | solution.py:80
  725.5 23.5 %all-reduce.8.cloned.1.call-done = (bf16[128,512]{0,1:T(8,128)(2,1)}, bf16[128,512]{0,1:T(8,128)(2,1)}) async-done(((bf16[128,512]{0,1:T(8,128)(2,1)}, bf16[128,512]{0,1:T(8,128)(2,1)}), (bf16[128,512]{0,1:T(8,128)(2,1)}, bf16[128,512]{0,1:T(8,128)(2,1)})) %all-reduce.8.cloned.1.call-update) | async-done | bytes 262160 | tf_op jit(solution)/shard_map/psum | solution.py:93
  (62 shorter events, 26.1 us)
Async XLA Ops:
  7.2 704.4 %copy-start = (f32[52,52]{1,0:T(8,128)S(1)}, f32[52,52]{1,0:T(8,128)}, u32[]{:S(2)}) copy-start(f32[52,52]{1,0:T(8,128)} %param.11) | copy-start | bytes 32452
  7.2 435.7 %all-reduce.6.cloned.1.call-start = ((), (), s32[]{:S(2)}) async-start(), calls=%async_computation.3 | async-start | bytes 7503872 | tf_op jit(solution)/shard_map/psum | solution.py:41
  7.2 78.4 %collective-permute-start = (bf16[26,128,512]{2,1,0:T(8,128)(2,1)}, bf16[26,128,512]{2,1,0:T(8,128)(2,1)S(1)}, u32[]{:S(2)}, u32[]{:S(2)}) collective-permute-start(bf16[26,128,512]{2,1,0:T(8,128)(2,1)} %param.7), channel_id=1, source_target_pairs={{0,3},{1,0},{2,1},{3,2},{4,7},{5,4},{6,5},{7,6},{8,11},{9,8},{10,9... | collective-permute-start | bytes 10223624 | tf_op jit(solution)/shard_map/ppermute | solution.py:29
  85.6 76.3 %collective-permute-start.1 = (bf16[26,128,512]{2,1,0:T(8,128)(2,1)S(1)}, bf16[26,128,512]{2,1,0:T(8,128)(2,1)}, u32[]{:S(2)}, u32[]{:S(2)}) collective-permute-start(bf16[26,128,512]{2,1,0:T(8,128)(2,1)S(1)} %collective-permute-done), channel_id=1, source_target_pairs={{0,3},{1,0},{2,1},{3,2},{4,7},{5,4},{6,5},{7,6},{8,11},{9,8},{10,9... | collective-permute-start | bytes 10223624 | tf_op jit(solution)/shard_map/ppermute | solution.py:29
  161.9 76.0 %collective-permute-start.2 = (bf16[26,128,512]{2,1,0:T(8,128)(2,1)}, bf16[26,128,512]{2,1,0:T(8,128)(2,1)}, u32[]{:S(2)}, u32[]{:S(2)}) collective-permute-start(bf16[26,128,512]{2,1,0:T(8,128)(2,1)} %collective-permute-done.1), channel_id=1, source_target_pairs={{0,3},{1,0},{2,1},{3,2},{4,7},{5,4},{6,5},{7,6},{8,11},{9,8},{10,9... | collective-permute-start | bytes 10223624 | tf_op jit(solution)/shard_map/ppermute | solution.py:29
  167.0 2.5 copy-start.4
  167.1 2.5 copy-start.6
  172.4 67.9 %copy-start.3 = (bf16[26,128,512]{2,1,0:T(8,128)(2,1)S(1)}, bf16[26,128,512]{2,1,0:T(8,128)(2,1)}, u32[]{:S(2)}) copy-start(bf16[26,128,512]{2,1,0:T(8,128)(2,1)} %param.7) | copy-start | bytes 10223620
  246.1 9.0 %copy-start.1 = (bf16[26,128,4096]{2,1,0:T(8,128)(2,1)}, bf16[26,128,4096]{2,1,0:T(8,128)(2,1)S(1)}, u32[]{:S(2)}) copy-start(bf16[26,128,4096]{2,1,0:T(8,128)(2,1)S(1)} %constant_dynamic-update-slice_fusion) | copy-start | bytes 81788928
  273.1 11.0 %copy-start.9 = (s32[26,128]{1,0:T(8,128)S(1)}, s32[26,128]{1,0:T(8,128)}, u32[]{:S(2)}) copy-start(s32[26,128]{1,0:T(8,128)} %param.9) | copy-start | bytes 39940
  273.1 11.1 %copy-start.7 = (bf16[26,128,128]{2,1,0:T(8,128)(2,1)S(1)}, bf16[26,128,128]{2,1,0:T(8,128)(2,1)}, u32[]{:S(2)}) copy-start(bf16[26,128,128]{2,1,0:T(8,128)(2,1)} %param.6) | copy-start | bytes 2555908
  273.1 11.6 %copy-start.5 = (f32[26,32,128]{2,1,0:T(8,128)S(1)}, f32[26,32,128]{2,1,0:T(8,128)}, u32[]{:S(2)}) copy-start(f32[26,32,128]{2,1,0:T(8,128)} %param.8) | copy-start | bytes 1277956
  283.9 334.7 %reduce-scatter.2.cloned.1.call-start = ((), (), s32[]{:S(2)}) async-start(), calls=%async_computation.1 | async-start | bytes 17039360 | tf_op jit(solution)/shard_map/reduce_scatter | solution.py:60
  442.9 6.7 copy-start.8
  442.9 19.3 %copy-start.2 = (bf16[26,128,4096]{2,1,0:T(8,128)(2,1)S(1)}, bf16[26,128,4096]{2,1,0:T(8,128)(2,1)}, u32[]{:S(2)}) copy-start(bf16[26,128,4096]{2,1,0:T(8,128)(2,1)} %copy-done.1) | copy-start | bytes 81788928
  511.7 0.7 copy-start.10
  511.7 199.8 %all-gather.2.cloned.1.call-start = ((), (), s32[]{:S(2)}) async-start(), calls=%async_computation.2 | async-start | bytes 10223616 | tf_op jit(solution)/shard_map/all_gather | solution.py:83
  625.1 123.9 %all-reduce.8.cloned.1.call-start = ((), (), s32[]{:S(2)}) async-start(), calls=%async_computation.4 | async-start | bytes 524288 | tf_op jit(solution)/shard_map/psum | solution.py:93
Sparse Core Ops, SparseCore 0:
  284.1 82.8 all-reduce.5
  511.8 106.7 reduce-scatter.1
  625.2 86.2 all-gather.1
  725.6 23.3 all-reduce.7
